TPU v7x, 32 devices: a whole 2x2x4 slice. The times are simulated.
32 devices in a mesh: heads: 2 (over core), tm: 16 (over z, y, x).
Axes of the slice: x: 2, y: 2, z: 4, core: 2. Of those that a mesh axis runs over, the one named last changes fastest.
Arguments:
- queries: bfloat16 [4096, 768], P('tm', 'heads'), parts along dimension 1, may hold values from -8 to 8
- keys: bfloat16 [4096, 768], P('tm', 'heads'), parts along dimension 1, may hold values from -8 to 8
- values: bfloat16 [4096, 768], P('tm', 'heads'), parts along dimension 1, may hold values from -6 to 6
- positions: int32 [3, 4096], P(None, 'tm'), may hold values from 0 to 79, as said below
- tile_masks: int32 [32, 8, 2], P('tm'), may hold values from 0 to 1, as said below
- sink_index: int32 [256], replicated, may hold values from 0 to 3599, as said below
Outputs:
- attended: bfloat16 [4096, 768], P('tm', 'heads'), parts along dimension 1
There are 2 independent parts, one for each index of `heads`. A program takes and returns all parts, laid end to end along the dimension named above; an argument that names none is the same for every part. Nothing has to cross between parts.
Inputs may be any that keep to these rules, and one draw needn't show every extreme that they name: `positions`: consecutive tokens of the latent video of 33 x 45 x 80, row by row, from some starting token. `tile_masks`: tiles of farther partners are kept less often. `sink_index`: distinct rows among the first min(4096, 3600) of the window.
All inputs are finite; a program needn't handle non-finite values.
Results may differ from a plain program's by a relative error of at most 0.0085.
The roundings to bfloat16 on the way count: a program that leaves them out, or rounds other values in their place, can miss the bound.
Values may be sent and summed in bfloat16 or wider, within the bound.
No kernel may reach another device: no remote copies, remote signals or barrier semaphores. Data moves between devices by JAX's collectives and lax.ppermute only.
A program may use at most 64 MiB of HBM per device.

v0:
```python
import jax
import jax.numpy as jnp
from jax import lax
from jax.sharding import PartitionSpec as P

HG = 3
HD = 128
TILE = 128
NOFF = 4
SINK = 256


def shifted(shard, axis, by):
    length = lax.axis_size(axis)
    pairs = [(i, i + by) for i in range(length) if 0 <= i + by < length]
    return lax.ppermute(shard, axis, pairs)


def rotate(row_data, position, factor):
    row_count = row_data.shape[0]
    first_size = HD // 8
    second_size = (HD - HD // 8) // 2
    section_sizes = (first_size, second_size, HD - first_size - second_size)
    angle_list = []
    for axis_id in range(3):
        section_width = section_sizes[axis_id]
        inverse = 256.0 ** (-jnp.arange(0, section_width, 2).astype(jnp.float32) / section_width)
        angle_list.append(position[axis_id].astype(jnp.float32)[:, None] * inverse[None, :])
    angle_all = jnp.concatenate(angle_list, axis=1)
    cosine = jnp.cos(angle_all)[:, None, :]
    sine_part = jnp.sin(angle_all)[:, None, :]
    pair_view = row_data.astype(jnp.float32).reshape(row_count, HG, HD // 2, 2)
    even_part = pair_view[..., 0]
    odd_part = pair_view[..., 1]
    turned = jnp.stack(
        [even_part * cosine - odd_part * sine_part, even_part * sine_part + odd_part * cosine],
        axis=-1,
    )
    return (turned * factor).reshape(row_count, HG * HD)


def block_part(query_heads, key_heads, value_heads, tile_keep):
    keep_mask = jnp.repeat(jnp.repeat(tile_keep, TILE, axis=0), TILE, axis=1)[:, None, :]
    scores = jnp.einsum("qhd,khd->qhk", query_heads, key_heads, preferred_element_type=jnp.float32)
    masked = jnp.where(keep_mask > 0, scores, -1e30)
    row_max = jnp.max(masked, axis=2)
    weights = jnp.exp(masked - row_max[:, :, None]) * keep_mask
    totals = jnp.sum(weights, axis=2)
    weighted = jnp.einsum(
        "qhk,khd->qhd",
        weights.astype(jnp.bfloat16),
        value_heads,
        preferred_element_type=jnp.float32,
    )
    return (weighted, row_max, totals)


def combine_parts(first, second):
    weighted_a, max_a, total_a = first
    weighted_b, max_b, total_b = second
    new_max = jnp.maximum(max_a, max_b)
    scale_first = jnp.exp(max_a - new_max)
    scale_second = jnp.exp(max_b - new_max)
    weighted = weighted_a * scale_first[:, :, None] + weighted_b * scale_second[:, :, None]
    return (weighted, new_max, total_a * scale_first + total_b * scale_second)


def on_device(queries, keys, values, positions, tile_masks, sink_index):
    rows_here = queries.shape[0]
    shards = lax.axis_size("tm")
    index_here = lax.axis_index("tm")
    feature_width = HG * HD
    tiles = rows_here // TILE
    q_rot = rotate(queries, positions, HD ** (-0.5)).astype(jnp.bfloat16)
    k_rot = rotate(keys, positions, 1.0).astype(jnp.bfloat16)
    query_heads = q_rot.reshape(rows_here, HG, HD)
    key_heads = k_rot.reshape(rows_here, HG, HD)
    value_heads = values.reshape(rows_here, HG, HD)
    state = block_part(query_heads, key_heads, value_heads, jnp.ones((tiles, tiles), jnp.float32))
    local_index = sink_index - index_here * rows_here
    one_hot = (local_index[:, None] == jnp.arange(rows_here, dtype=jnp.int32)[None, :]).astype(
        jnp.bfloat16
    )
    sink_table = jnp.dot(
        one_hot, jnp.concatenate([k_rot, values], axis=1), preferred_element_type=jnp.float32
    )
    sink_table = lax.psum(sink_table, "tm").astype(jnp.bfloat16)
    sink_keys = sink_table[:, :feature_width].reshape(SINK, HG, HD)
    sink_values = sink_table[:, feature_width:].reshape(SINK, HG, HD)
    sink_keep = jnp.ones((tiles, SINK // TILE), jnp.float32)
    state = combine_parts(state, block_part(query_heads, sink_keys, sink_values, sink_keep))
    mask_float = tile_masks.astype(jnp.float32)
    for offset in range(1, NOFF + 1):
        later_rows, later_values = shifted((k_rot, values), "tm", -offset)
        earlier_rows, earlier_values = shifted((k_rot, values), "tm", offset)
        later_ok = (index_here + offset < shards).astype(jnp.float32)
        earlier_ok = (index_here - offset >= 0).astype(jnp.float32)
        later_part = block_part(
            query_heads,
            later_rows.reshape(rows_here, HG, HD),
            later_values.reshape(rows_here, HG, HD),
            mask_float[:, offset - 1, :] * later_ok,
        )
        state = combine_parts(state, later_part)
        earlier_part = block_part(
            query_heads,
            earlier_rows.reshape(rows_here, HG, HD),
            earlier_values.reshape(rows_here, HG, HD),
            mask_float[:, NOFF + offset - 1, :] * earlier_ok,
        )
        state = combine_parts(state, earlier_part)
    weighted, row_max, totals = state
    return (weighted / totals[:, :, None]).astype(jnp.bfloat16).reshape(rows_here, feature_width)


def solution(mesh):
    in_specs = (
        P("tm", "heads"),
        P("tm", "heads"),
        P("tm", "heads"),
        P(None, "tm"),
        P("tm", None, None),
        P(),
    )
    out_specs = P("tm", "heads")
    return jax.shard_map(
        on_device, mesh=mesh, in_specs=in_specs, out_specs=out_specs, check_vma=False
    )
```

profile of v0, /device:TPU:0, one launch (start us, length us, event | category | flops | bytes accessed | tf_op | source)
XLA Modules:
  0.0 197.0 jit_solution(17712258259752564068)
XLA Ops:
  0.0 0.8 slice_convert_fusion.2
  0.8 1.1 copy.42
  3.6 5.8 %collective-permute-start.10 = (bf16[256,384]{0,1:T(8,128)(2,1)S(1)}, bf16[256,384]{0,1:T(8,128)(2,1)S(1)}, u32[]{:S(2)}, u32[]{:S(2)}) collective-permute-start(bf16[256,384]{0,1:T(8,128)(2,1)S(1)} %convert_element_type.149), channel_id=1, source_target_pairs={{0,3},{1,4},{2,5},{3,6},{4,7},{5,8},{6,9},{7,10},{8,11},{9,12},{10... | collective-permute-start | bytes 589832 | tf_op jit(solution)/shard_map/ppermute | solution.py:16
  9.4 1.3 collective-permute-start.8
  10.7 4.1 %collective-permute-start.6 = (bf16[256,384]{0,1:T(8,128)(2,1)S(1)}, bf16[256,384]{0,1:T(8,128)(2,1)}, u32[]{:S(2)}, u32[]{:S(2)}) collective-permute-start(bf16[256,384]{0,1:T(8,128)(2,1)S(1)} %convert_element_type.149), channel_id=1, source_target_pairs={{0,2},{1,3},{2,4},{3,5},{4,6},{5,7},{6,8},{7,9},{8,10},{9,11},{10,... | collective-permute-start | bytes 589832 | tf_op jit(solution)/shard_map/ppermute | solution.py:16
  14.8 1.3 collective-permute-start.4
  16.1 5.2 %collective-permute-start.2 = (bf16[256,384]{0,1:T(8,128)(2,1)S(1)}, bf16[256,384]{0,1:T(8,128)(2,1)}, u32[]{:S(2)}, u32[]{:S(2)}) collective-permute-start(bf16[256,384]{0,1:T(8,128)(2,1)S(1)} %convert_element_type.149), channel_id=1, source_target_pairs={{0,1},{1,2},{2,3},{3,4},{4,5},{5,6},{6,7},{7,8},{8,9},{9,10},{10,1... | collective-permute-start | bytes 589832 | tf_op jit(solution)/shard_map/ppermute | solution.py:16
  21.4 0.7 copy-done.65
  24.6 1.1 copy.46
  26.4 85.1 %all-reduce.1 = bf16[256,768]{1,0:T(8,128)(2,1)S(1)} all-reduce(f32[256,768]{1,0:T(8,128)S(1)} %fusion.68), channel_id=1, replica_groups=mesh['heads'=2,'tm'=16] {'tm'}, use_global_device_ids=true, to_apply=%region_1.2 | all-reduce | flops 196608 | bytes 1179648 | tf_op jit(solution)/shard_map/psum | solution.py:87
  117.8 0.8 copy.52
  118.9 1.3 collective-permute-start
  120.5 1.3 collective-permute-start.12
  121.9 1.3 fusion.102
  123.2 4.6 %collective-permute-start.14 = (bf16[256,384]{0,1:T(8,128)(2,1)S(1)}, bf16[256,384]{0,1:T(8,128)(2,1)S(1)}, u32[]{:S(2)}, u32[]{:S(2)}) collective-permute-start(bf16[256,384]{0,1:T(8,128)(2,1)S(1)} %convert_element_type.149), channel_id=1, source_target_pairs={{0,4},{1,5},{2,6},{3,7},{4,8},{5,9},{6,10},{7,11},{8,12},{9,13},{1... | collective-permute-start | bytes 589832 | tf_op jit(solution)/shard_map/ppermute | solution.py:16
  127.7 1.3 fusion.103
  129.1 4.5 %collective-permute-start.3 = (bf16[256,384]{1,0:T(8,128)(2,1)}, bf16[256,384]{1,0:T(8,128)(2,1)S(1)}, u32[]{:S(2)}, u32[]{:S(2)}) collective-permute-start(bf16[256,384]{1,0:T(8,128)(2,1)} %param.8), channel_id=1, source_target_pairs={{0,1},{1,2},{2,3},{3,4},{4,5},{5,6},{6,7},{7,8},{8,9},{9,10},{10,1... | collective-permute-start | bytes 589832 | tf_op jit(solution)/shard_map/ppermute | solution.py:16
  133.6 1.3 fusion.104
  135.0 1.3 collective-permute-start.5
  136.3 1.3 fusion.105
  137.6 5.2 %collective-permute-start.7 = (bf16[256,384]{1,0:T(8,128)(2,1)}, bf16[256,384]{1,0:T(8,128)(2,1)}, u32[]{:S(2)}, u32[]{:S(2)}) collective-permute-start(bf16[256,384]{1,0:T(8,128)(2,1)} %param.8), channel_id=1, source_target_pairs={{0,2},{1,3},{2,4},{3,5},{4,6},{5,7},{6,8},{7,9},{8,10},{9,11},{10,... | collective-permute-start | bytes 589832 | tf_op jit(solution)/shard_map/ppermute | solution.py:16
  143.2 1.3 collective-permute-start.9
  144.9 6.1 %collective-permute-start.11 = (bf16[256,384]{1,0:T(8,128)(2,1)}, bf16[256,384]{1,0:T(8,128)(2,1)}, u32[]{:S(2)}, u32[]{:S(2)}) collective-permute-start(bf16[256,384]{1,0:T(8,128)(2,1)} %param.8), channel_id=1, source_target_pairs={{0,3},{1,4},{2,5},{3,6},{4,7},{5,8},{6,9},{7,10},{8,11},{9,12},{10... | collective-permute-start | bytes 589832 | tf_op jit(solution)/shard_map/ppermute | solution.py:16
  151.4 0.7 copy-done.64
  155.5 0.7 copy-done.52
  157.6 0.7 copy-done.54
  161.6 1.0 fusion.30
  162.6 0.7 copy-done.37
  163.2 1.3 collective-permute-start.13
  164.5 1.1 copy.62
  165.6 2.2 %fusion.11 = f32[256,3,128]{0,2,1:T(8,128)} fusion(bf16[256,3,128]{0,2,1:T(8,128)(2,1)S(1)} %bitcast.276, f32[256,3,256]{0,2,1:T(8,128)} %copy-done.7, f32[256,256]{0,1:T(8,128)S(1)} %bitcast.272, f32[256,3]{0,1:T(4,128)S(1)} %copy-done.46, f32[256,3]{0,1:T(4,128)S(1)} %get-tuple-element.17), kind=kOutput, calls=%fused_computation.31 | convolution fusion | flops 51019776 | bytes 1644544 | tf_op jit(solution)/shard_map/qhk,khd->qhd/dot_general | solution.py:49
  167.8 5.2 %collective-permute-start.15 = (bf16[256,384]{1,0:T(8,128)(2,1)}, bf16[256,384]{1,0:T(8,128)(2,1)}, u32[]{:S(2)}, u32[]{:S(2)}) collective-permute-start(bf16[256,384]{1,0:T(8,128)(2,1)} %param.8), channel_id=1, source_target_pairs={{0,4},{1,5},{2,6},{3,7},{4,8},{5,9},{6,10},{7,11},{8,12},{9,13},{1... | collective-permute-start | bytes 589832 | tf_op jit(solution)/shard_map/ppermute | solution.py:16
  173.0 1.7 copy.67
  174.8 2.4 %fusion.12 = f32[256,3,128]{0,2,1:T(8,128)} fusion(bf16[256,3,128]{0,2,1:T(8,128)(2,1)} %bitcast.277, f32[256,3,256]{0,2,1:T(8,128)} %copy-done.6, f32[256,256]{0,1:T(8,128)} %bitcast.270, f32[256,3]{0,1:T(4,128)S(1)} %copy-done.44, f32[256,3]{0,1:T(4,128)S(1)} %get-tuple-element.18), kind=kOutput, calls=%fused_computation.32 | convolution fusion | flops 51019776 | bytes 1644544 | tf_op jit(solution)/shard_map/qhk,khd->qhd/dot_general | solution.py:49
  177.1 1.3 collective-permute-start.1
  178.4 1.7 copy.72
  180.2 2.1 %fusion.13 = f32[256,3,128]{0,2,1:T(8,128)} fusion(bf16[256,3,128]{0,2,1:T(8,128)(2,1)} %bitcast.278, f32[256,3,256]{0,2,1:T(8,128)S(1)} %copy-done.1, f32[256,256]{0,1:T(8,128)} %bitcast.268, f32[256,3]{0,1:T(4,128)S(1)} %copy-done.42, f32[256,3]{0,1:T(4,128)S(1)} %get-tuple-element.19), kind=kOutput, calls=%fused_computation.33 | convolution fusion | flops 51019776 | bytes 1644544 | tf_op jit(solution)/shard_map/qhk,khd->qhd/dot_general | solution.py:49
  182.3 1.1 copy.77
  183.4 1.0 fusion.14
  184.4 1.1 copy.82
  185.6 1.0 fusion.15
  186.6 1.1 copy.87
  187.7 1.0 fusion.16
  188.8 1.8 copy.92
  190.6 2.0 %fusion.17 = f32[256,3,128]{0,2,1:T(8,128)} fusion(bf16[256,3,128]{0,2,1:T(8,128)(2,1)} %bitcast.282, f32[256,3,256]{0,2,1:T(8,128)S(1)} %copy-done.5, f32[256,256]{0,1:T(8,128)S(1)} %bitcast.260, f32[256,3]{0,1:T(4,128)S(1)} %get-tuple-element.49, f32[256,3]{0,1:T(4,128)S(1)} %get-tuple-element.23), kind=kOutput, calls=%fused_computation.37 | convolution fusion | flops 51019776 | bytes 1644544 | tf_op jit(solution)/shard_map/qhk,khd->qhd/dot_general | solution.py:49
  192.6 1.1 copy.57
  194.4 1.8 fusion.36
  196.2 0.8 copy.94
  (220 shorter events, 21.5 us)
Async XLA Ops:
  3.6 115.3 %collective-permute-start.10 = (bf16[256,384]{0,1:T(8,128)(2,1)S(1)}, bf16[256,384]{0,1:T(8,128)(2,1)S(1)}, u32[]{:S(2)}, u32[]{:S(2)}) collective-permute-start(bf16[256,384]{0,1:T(8,128)(2,1)S(1)} %convert_element_type.149), channel_id=1, source_target_pairs={{0,3},{1,4},{2,5},{3,6},{4,7},{5,8},{6,9},{7,10},{8,11},{9,12},{10... | collective-permute-start | bytes 589832 | tf_op jit(solution)/shard_map/ppermute | solution.py:16
  9.4 111.1 %collective-permute-start.8 = (bf16[256,384]{0,1:T(8,128)(2,1)S(1)}, bf16[256,384]{0,1:T(8,128)(2,1)S(1)}, u32[]{:S(2)}, u32[]{:S(2)}) collective-permute-start(bf16[256,384]{0,1:T(8,128)(2,1)S(1)} %convert_element_type.149), channel_id=1, source_target_pairs={{3,0},{4,1},{5,2},{6,3},{7,4},{8,5},{9,6},{10,7},{11,8},{12,9},{13... | collective-permute-start | bytes 589832 | tf_op jit(solution)/shard_map/ppermute | solution.py:16
  10.7 112.4 %collective-permute-start.6 = (bf16[256,384]{0,1:T(8,128)(2,1)S(1)}, bf16[256,384]{0,1:T(8,128)(2,1)}, u32[]{:S(2)}, u32[]{:S(2)}) collective-permute-start(bf16[256,384]{0,1:T(8,128)(2,1)S(1)} %convert_element_type.149), channel_id=1, source_target_pairs={{0,2},{1,3},{2,4},{3,5},{4,6},{5,7},{6,8},{7,9},{8,10},{9,11},{10,... | collective-permute-start | bytes 589832 | tf_op jit(solution)/shard_map/ppermute | solution.py:16
  14.8 114.2 %collective-permute-start.4 = (bf16[256,384]{0,1:T(8,128)(2,1)S(1)}, bf16[256,384]{0,1:T(8,128)(2,1)}, u32[]{:S(2)}, u32[]{:S(2)}) collective-permute-start(bf16[256,384]{0,1:T(8,128)(2,1)S(1)} %convert_element_type.149), channel_id=1, source_target_pairs={{2,0},{3,1},{4,2},{5,3},{6,4},{7,5},{8,6},{9,7},{10,8},{11,9},{12,... | collective-permute-start | bytes 589832 | tf_op jit(solution)/shard_map/ppermute | solution.py:16
  16.1 118.8 %collective-permute-start.2 = (bf16[256,384]{0,1:T(8,128)(2,1)S(1)}, bf16[256,384]{0,1:T(8,128)(2,1)}, u32[]{:S(2)}, u32[]{:S(2)}) collective-permute-start(bf16[256,384]{0,1:T(8,128)(2,1)S(1)} %convert_element_type.149), channel_id=1, source_target_pairs={{0,1},{1,2},{2,3},{3,4},{4,5},{5,6},{6,7},{7,8},{8,9},{9,10},{10,1... | collective-permute-start | bytes 589832 | tf_op jit(solution)/shard_map/ppermute | solution.py:16
  112.0 6.7 %copy-start.8 = (f32[256,3,256]{0,2,1:T(8,128)}, f32[256,3,256]{0,2,1:T(8,128)S(1)}, u32[]{:S(2)}) copy-start(f32[256,3,256]{0,2,1:T(8,128)S(1)} %get-tuple-element.66) | copy-start | bytes 2359300
  118.9 18.7 %collective-permute-start = (bf16[256,384]{0,1:T(8,128)(2,1)S(1)}, bf16[256,384]{0,1:T(8,128)(2,1)S(1)}, u32[]{:S(2)}, u32[]{:S(2)}) collective-permute-start(bf16[256,384]{0,1:T(8,128)(2,1)S(1)} %convert_element_type.149), channel_id=1, source_target_pairs={{1,0},{2,1},{3,2},{4,3},{5,4},{6,5},{7,6},{8,7},{9,8},{10,9},{11,1... | collective-permute-start | bytes 589832 | tf_op jit(solution)/shard_map/ppermute | solution.py:16
  120.2 1.7 copy-start.35
  120.5 1.3 copy-start.36
  120.5 22.6 %collective-permute-start.12 = (bf16[256,384]{0,1:T(8,128)(2,1)S(1)}, bf16[256,384]{0,1:T(8,128)(2,1)S(1)}, u32[]{:S(2)}, u32[]{:S(2)}) collective-permute-start(bf16[256,384]{0,1:T(8,128)(2,1)S(1)} %convert_element_type.149), channel_id=1, source_target_pairs={{4,0},{5,1},{6,2},{7,3},{8,4},{9,5},{10,6},{11,7},{12,8},{13,9},{1... | collective-permute-start | bytes 589832 | tf_op jit(solution)/shard_map/ppermute | solution.py:16
  121.8 5.9 %copy-start.34 = (pred[256,256]{0,1:T(8,128)(4,1)S(1)}, pred[256,256]{0,1:T(8,128)(4,1)}, u32[]{:S(2)}) copy-start(pred[256,256]{0,1:T(8,128)(4,1)} %bitcast_compare_fusion.4) | copy-start | bytes 196612
  123.2 21.7 %collective-permute-start.14 = (bf16[256,384]{0,1:T(8,128)(2,1)S(1)}, bf16[256,384]{0,1:T(8,128)(2,1)S(1)}, u32[]{:S(2)}, u32[]{:S(2)}) collective-permute-start(bf16[256,384]{0,1:T(8,128)(2,1)S(1)} %convert_element_type.149), channel_id=1, source_target_pairs={{0,4},{1,5},{2,6},{3,7},{4,8},{5,9},{6,10},{7,11},{8,12},{9,13},{1... | collective-permute-start | bytes 589832 | tf_op jit(solution)/shard_map/ppermute | solution.py:16
  127.7 5.9 %copy-start.33 = (pred[256,256]{0,1:T(8,128)(4,1)S(1)}, pred[256,256]{0,1:T(8,128)(4,1)}, u32[]{:S(2)}) copy-start(pred[256,256]{0,1:T(8,128)(4,1)} %bitcast_compare_fusion.5) | copy-start | bytes 196612
  129.0 25.8 %copy-start = (f32[256,3,256]{0,2,1:T(8,128)}, f32[256,3,256]{0,2,1:T(8,128)S(1)}, u32[]{:S(2)}) copy-start(f32[256,3,256]{0,2,1:T(8,128)S(1)} %get-tuple-element.58) | copy-start | bytes 2359300
  129.0 30.6 %copy-start.41 = (f32[256,3]{0,1:T(4,128)}, f32[256,3]{0,1:T(4,128)S(1)}, u32[]{:S(2)}) copy-start(f32[256,3]{0,1:T(4,128)S(1)} %get-tuple-element.57) | copy-start | bytes 9220
  129.1 33.5 %collective-permute-start.3 = (bf16[256,384]{1,0:T(8,128)(2,1)}, bf16[256,384]{1,0:T(8,128)(2,1)S(1)}, u32[]{:S(2)}, u32[]{:S(2)}) collective-permute-start(bf16[256,384]{1,0:T(8,128)(2,1)} %param.8), channel_id=1, source_target_pairs={{0,1},{1,2},{2,3},{3,4},{4,5},{5,6},{6,7},{7,8},{8,9},{9,10},{10,1... | collective-permute-start | bytes 589832 | tf_op jit(solution)/shard_map/ppermute | solution.py:16
  133.6 2.6 %copy-start.32 = (pred[256,256]{0,1:T(8,128)(4,1)S(1)}, pred[256,256]{0,1:T(8,128)(4,1)}, u32[]{:S(2)}) copy-start(pred[256,256]{0,1:T(8,128)(4,1)} %bitcast_compare_fusion.6) | copy-start | bytes 196612
  134.9 19.9 %copy-start.6 = (f32[256,3,256]{0,2,1:T(8,128)}, f32[256,3,256]{0,2,1:T(8,128)S(1)}, u32[]{:S(2)}) copy-start(f32[256,3,256]{0,2,1:T(8,128)S(1)} %get-tuple-element.60) | copy-start | bytes 2359300
  134.9 24.7 %copy-start.43 = (f32[256,3]{0,1:T(4,128)}, f32[256,3]{0,1:T(4,128)S(1)}, u32[]{:S(2)}) copy-start(f32[256,3]{0,1:T(4,128)S(1)} %get-tuple-element.59) | copy-start | bytes 9220
  135.0 32.9 %collective-permute-start.5 = (bf16[256,384]{1,0:T(8,128)(2,1)}, bf16[256,384]{1,0:T(8,128)(2,1)}, u32[]{:S(2)}, u32[]{:S(2)}) collective-permute-start(bf16[256,384]{1,0:T(8,128)(2,1)} %param.8), channel_id=1, source_target_pairs={{2,0},{3,1},{4,2},{5,3},{6,4},{7,5},{8,6},{9,7},{10,8},{11,9},{12,... | collective-permute-start | bytes 589832 | tf_op jit(solution)/shard_map/ppermute | solution.py:16
  136.3 6.6 %copy-start.31 = (pred[256,256]{0,1:T(8,128)(4,1)S(1)}, pred[256,256]{0,1:T(8,128)(4,1)}, u32[]{:S(2)}) copy-start(pred[256,256]{0,1:T(8,128)(4,1)} %bitcast_compare_fusion.7) | copy-start | bytes 196612
  137.6 15.2 %copy-start.7 = (f32[256,3,256]{0,2,1:T(8,128)}, f32[256,3,256]{0,2,1:T(8,128)S(1)}, u32[]{:S(2)}) copy-start(f32[256,3,256]{0,2,1:T(8,128)S(1)} %get-tuple-element.62) | copy-start | bytes 2359300
  137.6 22.1 %copy-start.45 = (f32[256,3]{0,1:T(4,128)}, f32[256,3]{0,1:T(4,128)S(1)}, u32[]{:S(2)}) copy-start(f32[256,3]{0,1:T(4,128)S(1)} %get-tuple-element.61) | copy-start | bytes 9220
  137.6 39.6 %collective-permute-start.7 = (bf16[256,384]{1,0:T(8,128)(2,1)}, bf16[256,384]{1,0:T(8,128)(2,1)}, u32[]{:S(2)}, u32[]{:S(2)}) collective-permute-start(bf16[256,384]{1,0:T(8,128)(2,1)} %param.8), channel_id=1, source_target_pairs={{0,2},{1,3},{2,4},{3,5},{4,6},{5,7},{6,8},{7,9},{8,10},{9,11},{10,... | collective-permute-start | bytes 589832 | tf_op jit(solution)/shard_map/ppermute | solution.py:16
  142.8 1.6 copy-start.30
  143.2 16.5 %copy-start.39 = (f32[256,3]{0,1:T(4,128)}, f32[256,3]{0,1:T(4,128)S(1)}, u32[]{:S(2)}) copy-start(f32[256,3]{0,1:T(4,128)S(1)} %get-tuple-element.63) | copy-start | bytes 9220
  143.2 39.1 %collective-permute-start.9 = (bf16[256,384]{1,0:T(8,128)(2,1)}, bf16[256,384]{1,0:T(8,128)(2,1)}, u32[]{:S(2)}, u32[]{:S(2)}) collective-permute-start(bf16[256,384]{1,0:T(8,128)(2,1)} %param.8), channel_id=1, source_target_pairs={{3,0},{4,1},{5,2},{6,3},{7,4},{8,5},{9,6},{10,7},{11,8},{12,9},{13... | collective-permute-start | bytes 589832 | tf_op jit(solution)/shard_map/ppermute | solution.py:16
  144.5 6.5 %copy-start.29 = (pred[256,256]{0,1:T(8,128)(4,1)S(1)}, pred[256,256]{0,1:T(8,128)(4,1)}, u32[]{:S(2)}) copy-start(pred[256,256]{0,1:T(8,128)(4,1)} %bitcast_compare_fusion) | copy-start | bytes 196612
  144.8 14.1 %copy-start.2 = (f32[256,3,256]{0,2,1:T(8,128)}, f32[256,3,256]{0,2,1:T(8,128)S(1)}, u32[]{:S(2)}) copy-start(f32[256,3,256]{0,2,1:T(8,128)S(1)} %get-tuple-element.52) | copy-start | bytes 2359300
  144.8 14.8 %copy-start.47 = (f32[256,3]{0,1:T(4,128)}, f32[256,3]{0,1:T(4,128)S(1)}, u32[]{:S(2)}) copy-start(f32[256,3]{0,1:T(4,128)S(1)} %get-tuple-element.51) | copy-start | bytes 9220
  144.9 39.6 %collective-permute-start.11 = (bf16[256,384]{1,0:T(8,128)(2,1)}, bf16[256,384]{1,0:T(8,128)(2,1)}, u32[]{:S(2)}, u32[]{:S(2)}) collective-permute-start(bf16[256,384]{1,0:T(8,128)(2,1)} %param.8), channel_id=1, source_target_pairs={{0,3},{1,4},{2,5},{3,6},{4,7},{5,8},{6,9},{7,10},{8,11},{9,12},{10... | collective-permute-start | bytes 589832 | tf_op jit(solution)/shard_map/ppermute | solution.py:16
  151.3 7.6 %copy-start.4 = (f32[256,3,256]{0,2,1:T(8,128)}, f32[256,3,256]{0,2,1:T(8,128)S(1)}, u32[]{:S(2)}) copy-start(f32[256,3,256]{0,2,1:T(8,128)S(1)} %get-tuple-element.50) | copy-start | bytes 2359300
  159.0 1.2 copy-start.9
  162.6 3.1 %copy-start.21 = (f32[256,2,128]{0,2,1:T(8,128)S(1)}, f32[256,2,128]{0,2,1:T(8,128)}, u32[]{:S(2)}) copy-start(f32[256,2,128]{0,2,1:T(8,128)} %copy-done.20) | copy-start | bytes 786436
  163.2 23.3 %collective-permute-start.13 = (bf16[256,384]{1,0:T(8,128)(2,1)}, bf16[256,384]{1,0:T(8,128)(2,1)}, u32[]{:S(2)}, u32[]{:S(2)}) collective-permute-start(bf16[256,384]{1,0:T(8,128)(2,1)} %param.8), channel_id=1, source_target_pairs={{4,0},{5,1},{6,2},{7,3},{8,4},{9,5},{10,6},{11,7},{12,8},{13,9},{1... | collective-permute-start | bytes 589832 | tf_op jit(solution)/shard_map/ppermute | solution.py:16
  167.8 20.9 %collective-permute-start.15 = (bf16[256,384]{1,0:T(8,128)(2,1)}, bf16[256,384]{1,0:T(8,128)(2,1)}, u32[]{:S(2)}, u32[]{:S(2)}) collective-permute-start(bf16[256,384]{1,0:T(8,128)(2,1)} %param.8), channel_id=1, source_target_pairs={{0,4},{1,5},{2,6},{3,7},{4,8},{5,9},{6,10},{7,11},{8,12},{9,13},{1... | collective-permute-start | bytes 589832 | tf_op jit(solution)/shard_map/ppermute | solution.py:16
  173.0 1.7 copy-start.44
  174.8 5.4 %copy-start.1 = (f32[256,3,256]{0,2,1:T(8,128)S(1)}, f32[256,3,256]{0,2,1:T(8,128)}, u32[]{:S(2)}) copy-start(f32[256,3,256]{0,2,1:T(8,128)} %copy-done) | copy-start | bytes 2359300
  177.1 15.5 %collective-permute-start.1 = (bf16[256,384]{1,0:T(8,128)(2,1)}, bf16[256,384]{1,0:T(8,128)(2,1)}, u32[]{:S(2)}, u32[]{:S(2)}) collective-permute-start(bf16[256,384]{1,0:T(8,128)(2,1)} %param.8), channel_id=1, source_target_pairs={{1,0},{2,1},{3,2},{4,3},{5,4},{6,5},{7,6},{8,7},{9,8},{10,9},{11,1... | collective-permute-start | bytes 589832 | tf_op jit(solution)/shard_map/ppermute | solution.py:16
  178.4 1.8 copy-start.42
  185.5 2.1 %copy-start.3 = (f32[256,3,256]{0,2,1:T(8,128)S(1)}, f32[256,3,256]{0,2,1:T(8,128)}, u32[]{:S(2)}) copy-start(f32[256,3,256]{0,2,1:T(8,128)} %copy-done.2) | copy-start | bytes 2359300
  186.6 1.1 copy-start.48
  187.7 2.8 %copy-start.5 = (f32[256,3,256]{0,2,1:T(8,128)S(1)}, f32[256,3,256]{0,2,1:T(8,128)}, u32[]{:S(2)}) copy-start(f32[256,3,256]{0,2,1:T(8,128)} %copy-done.4) | copy-start | bytes 2359300
  188.7 1.8 copy-start.11
  190.5 3.2 %copy-start.25 = (f32[256,3,128]{0,2,1:T(8,128)S(1)}, f32[256,3,128]{0,2,1:T(8,128)}, u32[]{:S(2)}) copy-start(f32[256,3,128]{0,2,1:T(8,128)} %fusion.11) | copy-start | bytes 1179652
  190.5 3.2 %copy-start.26 = (f32[256,3,128]{0,2,1:T(8,128)S(1)}, f32[256,3,128]{0,2,1:T(8,128)}, u32[]{:S(2)}) copy-start(f32[256,3,128]{0,2,1:T(8,128)} %fusion.12) | copy-start | bytes 1179652
  190.5 3.2 %copy-start.27 = (f32[256,3,128]{0,2,1:T(8,128)S(1)}, f32[256,3,128]{0,2,1:T(8,128)}, u32[]{:S(2)}) copy-start(f32[256,3,128]{0,2,1:T(8,128)} %fusion.13) | copy-start | bytes 1179652
  192.6 1.2 copy-start.24
  (35 other events, 27.5 us)
where the time goes:
time: 198 us; the launch traced here: 197 us
  blocking collectives  85.1 us (43%)
  starting transfers between devices  51.1 us (26%)
  local copies, waits for them, and re-layouts  28.5 us (14%)
  matrix products  22.2 us (11%)
  other arithmetic  9.08 us (5%)
    psum x1, blocking collectives, on_device(): sink_table = lax.psum(sink_table, 'tm').astype(jnp.bfloat16)  85.1 us
    ppermute x16, starting transfers between devices, shifted(): return lax.ppermute(shard, axis, pairs)  51.1 us
    dot_general x10, matrix products, block_part(): jnp.einsum('qhk,khd->qhd', weights.astype(jnp.bfloat16), value_heads, pre...  14.8 us
    unnamed x151, local copies, waits for them, and re-layouts  13.1 us
    ppermute x8, local copies, waits for them, and re-layouts, shifted(): return lax.ppermute(shard, axis, pairs)  10.8 us
    dot_general x10, matrix products, block_part(): jnp.einsum('qhd,khd->qhk', query_heads, key_heads, preferred_element_type...  7.07 us
    gt x8, other arithmetic, block_part(): masked = jnp.where(keep_mask > 0, scores, -1e+30)  4.55 us
  transfers between devices with their start and end apart: 16, of which 0 were waited for; matrix products, arithmetic and copies ran while one was open for 21% of the time, Pallas kernels for 0%

commit v1 on v0

--- a/solution.py
+++ b/solution.py
@@ -84,7 +84,7 @@
     sink_table = jnp.dot(
         one_hot, jnp.concatenate([k_rot, values], axis=1), preferred_element_type=jnp.float32
     )
-    sink_table = lax.psum(sink_table, "tm").astype(jnp.bfloat16)
+    sink_table = jnp.sum(lax.all_gather(sink_table, "tm"), axis=0).astype(jnp.bfloat16)
     sink_keys = sink_table[:, :feature_width].reshape(SINK, HG, HD)
     sink_values = sink_table[:, feature_width:].reshape(SINK, HG, HD)
     sink_keep = jnp.ones((tiles, SINK // TILE), jnp.float32)

time: 198 us -> 234 us (1.18)
  waiting for transfers between devices: 0.04 us -> 96.6 us
  blocking collectives: 85.1 us -> 0 us
  between operations: 0.98 us -> 14.3 us
  other arithmetic: 9.08 us -> 20 us
  local copies, waits for them, and re-layouts: 28.5 us -> 23.5 us
  starting transfers between devices: 51.1 us -> 55.2 us
    psum x1 -> x0, blocking collectives: 85.1 us -> none  [on_device(): sink_table = lax.psum(sink_table, 'tm').astype(jnp.bfloat16)]
    all_gather x0 -> x1, waiting for transfers between devices: none -> 81.9 us  [on_device(): lax.all_gather(sink_table, 'tm')]
    ppermute x16, waiting for transfers between devices: 0.04 us -> 14.7 us  [shifted(): return lax.ppermute(shard, axis, pairs)]
    unnamed x151 -> x95, local copies, waits for them, and re-layouts: 13.1 us -> 2.74 us
    reduce_sum x0 -> x1, other arithmetic: none -> 6.21 us  [on_device(): jnp.sum(lax.all_gather(sink_table, 'tm'), axis=0).astype(jnp.bfloat16)]
    ppermute x16, starting transfers between devices: 51.1 us -> 55.2 us  [shifted(): return lax.ppermute(shard, axis, pairs)]
    dot_general x10, matrix products: 14.8 us -> 11.1 us  [block_part(): jnp.einsum('qhk,khd->qhd', weights.astype(jnp.bfloat16), value_heads, pre...]
    reduce_sum x5, other arithmetic: 1.35 us -> 4.97 us  [block_part(): totals = jnp.sum(weights, axis=2)]
  transfers between devices with their start and end apart: 16 -> 17, of which waited for: 0 -> 4; matrix products, arithmetic and copies ran while one was open for 21% -> 12% of each run, Pallas kernels for 0% -> 0%
where the time goes in v1:
time: 234 us; the launch traced here: 232 us
  waiting for transfers between devices  96.6 us (41%)
  starting transfers between devices  55.2 us (24%)
  local copies, waits for them, and re-layouts  23.5 us (10%)
  matrix products  22.8 us (10%)
  other arithmetic  20 us (9%)
  between operations  14.3 us (6%)
    all_gather x1, waiting for transfers between devices, on_device(): lax.all_gather(sink_table, 'tm')  81.9 us
    ppermute x16, starting transfers between devices, shifted(): return lax.ppermute(shard, axis, pairs)  55.2 us
    ppermute x16, waiting for transfers between devices, shifted(): return lax.ppermute(shard, axis, pairs)  14.7 us
    dot_general x10, matrix products, block_part(): jnp.einsum('qhk,khd->qhd', weights.astype(jnp.bfloat16), value_heads, pre...  11.1 us
    dot_general x10, matrix products, block_part(): jnp.einsum('qhd,khd->qhk', query_heads, key_heads, preferred_element_type...  9.48 us
    ppermute x8, local copies, waits for them, and re-layouts, shifted(): return lax.ppermute(shard, axis, pairs)  7.47 us
    reduce_sum x1, other arithmetic, on_device(): jnp.sum(lax.all_gather(sink_table, 'tm'), axis=0).astype(jnp.bfloat16)  6.21 us
    reduce_sum x5, other arithmetic, block_part(): totals = jnp.sum(weights, axis=2)  4.97 us
  transfers between devices with their start and end apart: 17, of which 4 were waited for; matrix products, arithmetic and copies ran while one was open for 12% of the time, Pallas kernels for 0%

profile of v1, /device:TPU:0, one launch (start us, length us, event | category | flops | bytes accessed | tf_op | source)
XLA Modules:
  0.0 232.3 jit_solution(11326038386474494109)
XLA Ops:
  7.4 1.1 copy.91
  10.8 1.1 copy.95
  12.6 2.1 fusion.68
  14.7 5.8 %collective-permute-start.10 = (bf16[256,384]{0,1:T(8,128)(2,1)}, bf16[256,384]{0,1:T(8,128)(2,1)S(1)}, u32[]{:S(2)}, u32[]{:S(2)}) collective-permute-start(bf16[256,384]{0,1:T(8,128)(2,1)} %convert_element_type.149), channel_id=1, source_target_pairs={{0,3},{1,4},{2,5},{3,6},{4,7},{5,8},{6,9},{7,10},{8,11},{9,12},{10... | collective-permute-start | bytes 589832 | tf_op jit(solution)/shard_map/ppermute | solution.py:16
  20.6 2.5 %collective-permute-start.3 = (bf16[256,384]{1,0:T(8,128)(2,1)}, bf16[256,384]{1,0:T(8,128)(2,1)S(1)}, u32[]{:S(2)}, u32[]{:S(2)}) collective-permute-start(bf16[256,384]{1,0:T(8,128)(2,1)} %param.8), channel_id=1, source_target_pairs={{0,1},{1,2},{2,3},{3,4},{4,5},{5,6},{6,7},{7,8},{8,9},{9,10},{10,1... | collective-permute-start | bytes 589832 | tf_op jit(solution)/shard_map/ppermute | solution.py:16
  23.1 1.3 collective-permute-start.5
  24.4 4.6 %collective-permute-start.7 = (bf16[256,384]{1,0:T(8,128)(2,1)}, bf16[256,384]{1,0:T(8,128)(2,1)S(1)}, u32[]{:S(2)}, u32[]{:S(2)}) collective-permute-start(bf16[256,384]{1,0:T(8,128)(2,1)} %param.8), channel_id=1, source_target_pairs={{0,2},{1,3},{2,4},{3,5},{4,6},{5,7},{6,8},{7,9},{8,10},{9,11},{10,... | collective-permute-start | bytes 589832 | tf_op jit(solution)/shard_map/ppermute | solution.py:16
  28.9 1.3 collective-permute-start.9
  31.3 1.1 copy.92
  37.5 7.4 %collective-permute-start.11 = (bf16[256,384]{1,0:T(8,128)(2,1)}, bf16[256,384]{1,0:T(8,128)(2,1)}, u32[]{:S(2)}, u32[]{:S(2)}) collective-permute-start(bf16[256,384]{1,0:T(8,128)(2,1)} %param.8), channel_id=1, source_target_pairs={{0,3},{1,4},{2,5},{3,6},{4,7},{5,8},{6,9},{7,10},{8,11},{9,12},{10... | collective-permute-start | bytes 589832 | tf_op jit(solution)/shard_map/ppermute | solution.py:16
  45.0 1.3 collective-permute-start.13
  46.2 7.0 %collective-permute-start.15 = (bf16[256,384]{1,0:T(8,128)(2,1)}, bf16[256,384]{1,0:T(8,128)(2,1)S(1)}, u32[]{:S(2)}, u32[]{:S(2)}) collective-permute-start(bf16[256,384]{1,0:T(8,128)(2,1)} %param.8), channel_id=1, source_target_pairs={{0,4},{1,5},{2,6},{3,7},{4,8},{5,9},{6,10},{7,11},{8,12},{9,13},{1... | collective-permute-start | bytes 589832 | tf_op jit(solution)/shard_map/ppermute | solution.py:16
  53.4 1.3 collective-permute-start.1
  58.2 1.3 collective-permute-start.8
  59.5 1.7 copy.131
  61.3 2.5 %collective-permute-done.13 = bf16[256,384]{1,0:T(8,128)(2,1)S(1)} collective-permute-done((bf16[256,384]{1,0:T(8,128)(2,1)}, bf16[256,384]{1,0:T(8,128)(2,1)S(1)}, u32[]{:S(2)}, u32[]{:S(2)}) %collective-permute-start.13) | collective-permute-done | bytes 196640 | tf_op jit(solution)/shard_map/ppermute | solution.py:16
  63.8 3.6 %collective-permute-start.6 = (bf16[256,384]{0,1:T(8,128)(2,1)}, bf16[256,384]{0,1:T(8,128)(2,1)S(1)}, u32[]{:S(2)}, u32[]{:S(2)}) collective-permute-start(bf16[256,384]{0,1:T(8,128)(2,1)} %convert_element_type.149), channel_id=1, source_target_pairs={{0,2},{1,3},{2,4},{3,5},{4,6},{5,7},{6,8},{7,9},{8,10},{9,11},{10,... | collective-permute-start | bytes 589832 | tf_op jit(solution)/shard_map/ppermute | solution.py:16
  68.2 1.3 collective-permute-start.4
  70.4 5.2 %collective-permute-start.2 = (bf16[256,384]{0,1:T(8,128)(2,1)}, bf16[256,384]{0,1:T(8,128)(2,1)}, u32[]{:S(2)}, u32[]{:S(2)}) collective-permute-start(bf16[256,384]{0,1:T(8,128)(2,1)} %convert_element_type.149), channel_id=1, source_target_pairs={{0,1},{1,2},{2,3},{3,4},{4,5},{5,6},{6,7},{7,8},{8,9},{9,10},{10,1... | collective-permute-start | bytes 589832 | tf_op jit(solution)/shard_map/ppermute | solution.py:16
  75.6 0.8 copy.106
  76.5 1.4 collective-permute-start
  78.3 1.3 collective-permute-start.12
  79.6 1.2 fusion.102
  80.8 8.6 %collective-permute-start.14 = (bf16[256,384]{0,1:T(8,128)(2,1)}, bf16[256,384]{0,1:T(8,128)(2,1)S(1)}, u32[]{:S(2)}, u32[]{:S(2)}) collective-permute-start(bf16[256,384]{0,1:T(8,128)(2,1)} %convert_element_type.149), channel_id=1, source_target_pairs={{0,4},{1,5},{2,6},{3,7},{4,8},{5,9},{6,10},{7,11},{8,12},{9,13},{1... | collective-permute-start | bytes 589832 | tf_op jit(solution)/shard_map/ppermute | solution.py:16
  89.7 1.5 fusion.105
  91.2 3.0 %collective-permute-done = bf16[256,384]{0,1:T(8,128)(2,1)S(1)} collective-permute-done((bf16[256,384]{0,1:T(8,128)(2,1)}, bf16[256,384]{0,1:T(8,128)(2,1)S(1)}, u32[]{:S(2)}, u32[]{:S(2)}) %collective-permute-start) | collective-permute-done | bytes 196640 | tf_op jit(solution)/shard_map/ppermute | solution.py:16
  94.2 1.2 fusion.106
  96.8 0.9 fusion.41
  97.7 1.3 fusion.104
  100.4 0.9 fusion.45
  101.3 9.1 %collective-permute-done.12 = bf16[256,384]{0,1:T(8,128)(2,1)S(1)} collective-permute-done((bf16[256,384]{0,1:T(8,128)(2,1)}, bf16[256,384]{0,1:T(8,128)(2,1)S(1)}, u32[]{:S(2)}, u32[]{:S(2)}) %collective-permute-start.12) | collective-permute-done | bytes 196640 | tf_op jit(solution)/shard_map/ppermute | solution.py:16
  110.8 1.0 fusion.49
  113.2 0.9 fusion.53
  114.1 81.9 %all-gather.3.cloned.1.call-done = f32[4096,768]{1,0:T(8,128)} async-done(((f32[256,768]{1,0:T(8,128)}), f32[4096,768]{1,0:T(8,128)}) %all-gather.3.cloned.1.call-update) | async-done | bytes 12582928 | tf_op jit(solution)/shard_map/all_gather | solution.py:87
  196.1 6.2 %reduce_sum.99 = bf16[256,768]{1,0:T(8,128)(2,1)} reduce(f32[16,256,768]{2,1,0:T(8,128)} %bitcast.258, f32[]{:T(128)} %constant.13.clone.1), dimensions={0}, to_apply=%region_1.2 | reduce | flops 2949120 | bytes 12976132 | tf_op jit(solution)/shard_map/reduce_sum | solution.py:87
  202.3 1.8 fusion.98
  204.1 1.7 copy.98
  205.8 2.7 %fusion.107 = (f32[256,3]{0,1:T(4,128)}, f32[256,3,256]{0,2,1:T(8,128)}) fusion(bf16[256,3,128]{0,2,1:T(8,128)(2,1)} %bitcast.285, bf16[256,3,128]{0,2,1:T(8,128)(2,1)S(1)} %convert_element_type.147), kind=kOutput, calls=%fused_computation.196 | convolution fusion | flops 50527488 | bytes 1182720 | tf_op jit(solution)/shard_map/qhd,khd->qhk/dot_general | solution.py:44
  208.5 1.8 copy.101
  211.1 1.4 fusion.37
  212.5 0.9 multiply_add_fusion.2
  213.4 1.4 fusion.8
  214.8 1.5 fusion.11
  216.3 1.5 fusion.12
  217.8 1.5 fusion.13
  219.4 1.3 fusion.14
  220.7 1.3 fusion.15
  222.0 1.5 fusion.16
  (167 shorter events, 23.0 us)
Async XLA Ops:
  6.5 189.5 %all-gather.3.cloned.1.call-start = ((), (), s32[]{:S(2)}) async-start(), calls=%async_computation | async-start | bytes 13369344 | tf_op jit(solution)/shard_map/all_gather | solution.py:87
  14.7 61.7 %collective-permute-start.10 = (bf16[256,384]{0,1:T(8,128)(2,1)}, bf16[256,384]{0,1:T(8,128)(2,1)S(1)}, u32[]{:S(2)}, u32[]{:S(2)}) collective-permute-start(bf16[256,384]{0,1:T(8,128)(2,1)} %convert_element_type.149), channel_id=1, source_target_pairs={{0,3},{1,4},{2,5},{3,6},{4,7},{5,8},{6,9},{7,10},{8,11},{9,12},{10... | collective-permute-start | bytes 589832 | tf_op jit(solution)/shard_map/ppermute | solution.py:16
  20.6 16.9 %collective-permute-start.3 = (bf16[256,384]{1,0:T(8,128)(2,1)}, bf16[256,384]{1,0:T(8,128)(2,1)S(1)}, u32[]{:S(2)}, u32[]{:S(2)}) collective-permute-start(bf16[256,384]{1,0:T(8,128)(2,1)} %param.8), channel_id=1, source_target_pairs={{0,1},{1,2},{2,3},{3,4},{4,5},{5,6},{6,7},{7,8},{8,9},{9,10},{10,1... | collective-permute-start | bytes 589832 | tf_op jit(solution)/shard_map/ppermute | solution.py:16
  23.1 21.9 %collective-permute-start.5 = (bf16[256,384]{1,0:T(8,128)(2,1)}, bf16[256,384]{1,0:T(8,128)(2,1)S(1)}, u32[]{:S(2)}, u32[]{:S(2)}) collective-permute-start(bf16[256,384]{1,0:T(8,128)(2,1)} %param.8), channel_id=1, source_target_pairs={{2,0},{3,1},{4,2},{5,3},{6,4},{7,5},{8,6},{9,7},{10,8},{11,9},{12,... | collective-permute-start | bytes 589832 | tf_op jit(solution)/shard_map/ppermute | solution.py:16
  24.4 21.9 %collective-permute-start.7 = (bf16[256,384]{1,0:T(8,128)(2,1)}, bf16[256,384]{1,0:T(8,128)(2,1)S(1)}, u32[]{:S(2)}, u32[]{:S(2)}) collective-permute-start(bf16[256,384]{1,0:T(8,128)(2,1)} %param.8), channel_id=1, source_target_pairs={{0,2},{1,3},{2,4},{3,5},{4,6},{5,7},{6,8},{7,9},{8,10},{9,11},{10,... | collective-permute-start | bytes 589832 | tf_op jit(solution)/shard_map/ppermute | solution.py:16
  28.9 24.3 %collective-permute-start.9 = (bf16[256,384]{1,0:T(8,128)(2,1)}, bf16[256,384]{1,0:T(8,128)(2,1)S(1)}, u32[]{:S(2)}, u32[]{:S(2)}) collective-permute-start(bf16[256,384]{1,0:T(8,128)(2,1)} %param.8), channel_id=1, source_target_pairs={{3,0},{4,1},{5,2},{6,3},{7,4},{8,5},{9,6},{10,7},{11,8},{12,9},{13... | collective-permute-start | bytes 589832 | tf_op jit(solution)/shard_map/ppermute | solution.py:16
  31.3 22.0 %copy-start.27 = (f32[1,2,2,128]{3,1,2,0:T(2,128)}, f32[1,2,2,128]{3,1,2,0:T(2,128)S(1)}, u32[]{:S(2)}) copy-start(f32[1,2,2,128]{3,1,2,0:T(2,128)S(1)} %copy.200) | copy-start | bytes 6148
  33.8 19.5 %copy-start.29 = (f32[1,2,2,128]{3,1,2,0:T(2,128)}, f32[1,2,2,128]{3,1,2,0:T(2,128)S(1)}, u32[]{:S(2)}) copy-start(f32[1,2,2,128]{3,1,2,0:T(2,128)S(1)} %copy.201) | copy-start | bytes 6148
  34.0 2.0 copy-start.33
  34.2 2.6 %copy-start.36 = (f32[1,2,2,128]{3,1,2,0:T(2,128)}, f32[1,2,2,128]{3,1,2,0:T(2,128)S(1)}, u32[]{:S(2)}) copy-start(f32[1,2,2,128]{3,1,2,0:T(2,128)S(1)} %copy.203) | copy-start | bytes 6148
  35.0 18.3 %copy-start.37 = (f32[1,2,2,128]{3,1,2,0:T(2,128)}, f32[1,2,2,128]{3,1,2,0:T(2,128)S(1)}, u32[]{:S(2)}) copy-start(f32[1,2,2,128]{3,1,2,0:T(2,128)S(1)} %copy.204) | copy-start | bytes 6148
  35.2 18.1 %copy-start.38 = (f32[1,2,2,128]{3,1,2,0:T(2,128)}, f32[1,2,2,128]{3,1,2,0:T(2,128)S(1)}, u32[]{:S(2)}) copy-start(f32[1,2,2,128]{3,1,2,0:T(2,128)S(1)} %copy.205) | copy-start | bytes 6148
  36.0 17.3 %copy-start.31 = (f32[1,2,2,128]{3,1,2,0:T(2,128)}, f32[1,2,2,128]{3,1,2,0:T(2,128)S(1)}, u32[]{:S(2)}) copy-start(f32[1,2,2,128]{3,1,2,0:T(2,128)S(1)} %copy.199) | copy-start | bytes 6148
  36.8 16.5 %copy-start.34 = (f32[1,2,2,128]{3,1,2,0:T(2,128)}, f32[1,2,2,128]{3,1,2,0:T(2,128)S(1)}, u32[]{:S(2)}) copy-start(f32[1,2,2,128]{3,1,2,0:T(2,128)S(1)} %copy.198) | copy-start | bytes 6148
  37.5 20.7 %collective-permute-start.11 = (bf16[256,384]{1,0:T(8,128)(2,1)}, bf16[256,384]{1,0:T(8,128)(2,1)}, u32[]{:S(2)}, u32[]{:S(2)}) collective-permute-start(bf16[256,384]{1,0:T(8,128)(2,1)} %param.8), channel_id=1, source_target_pairs={{0,3},{1,4},{2,5},{3,6},{4,7},{5,8},{6,9},{7,10},{8,11},{9,12},{10... | collective-permute-start | bytes 589832 | tf_op jit(solution)/shard_map/ppermute | solution.py:16
  45.0 18.9 %collective-permute-start.13 = (bf16[256,384]{1,0:T(8,128)(2,1)}, bf16[256,384]{1,0:T(8,128)(2,1)S(1)}, u32[]{:S(2)}, u32[]{:S(2)}) collective-permute-start(bf16[256,384]{1,0:T(8,128)(2,1)} %param.8), channel_id=1, source_target_pairs={{4,0},{5,1},{6,2},{7,3},{8,4},{9,5},{10,6},{11,7},{12,8},{13,9},{1... | collective-permute-start | bytes 589832 | tf_op jit(solution)/shard_map/ppermute | solution.py:16
  46.2 22.0 %collective-permute-start.15 = (bf16[256,384]{1,0:T(8,128)(2,1)}, bf16[256,384]{1,0:T(8,128)(2,1)S(1)}, u32[]{:S(2)}, u32[]{:S(2)}) collective-permute-start(bf16[256,384]{1,0:T(8,128)(2,1)} %param.8), channel_id=1, source_target_pairs={{0,4},{1,5},{2,6},{3,7},{4,8},{5,9},{6,10},{7,11},{8,12},{9,13},{1... | collective-permute-start | bytes 589832 | tf_op jit(solution)/shard_map/ppermute | solution.py:16
  53.4 17.0 %collective-permute-start.1 = (bf16[256,384]{1,0:T(8,128)(2,1)}, bf16[256,384]{1,0:T(8,128)(2,1)S(1)}, u32[]{:S(2)}, u32[]{:S(2)}) collective-permute-start(bf16[256,384]{1,0:T(8,128)(2,1)} %param.8), channel_id=1, source_target_pairs={{1,0},{2,1},{3,2},{4,3},{5,4},{6,5},{7,6},{8,7},{9,8},{10,9},{11,1... | collective-permute-start | bytes 589832 | tf_op jit(solution)/shard_map/ppermute | solution.py:16
  58.2 20.0 %collective-permute-start.8 = (bf16[256,384]{0,1:T(8,128)(2,1)}, bf16[256,384]{0,1:T(8,128)(2,1)S(1)}, u32[]{:S(2)}, u32[]{:S(2)}) collective-permute-start(bf16[256,384]{0,1:T(8,128)(2,1)} %convert_element_type.149), channel_id=1, source_target_pairs={{3,0},{4,1},{5,2},{6,3},{7,4},{8,5},{9,6},{10,7},{11,8},{12,9},{13... | collective-permute-start | bytes 589832 | tf_op jit(solution)/shard_map/ppermute | solution.py:16
  63.8 17.0 %collective-permute-start.6 = (bf16[256,384]{0,1:T(8,128)(2,1)}, bf16[256,384]{0,1:T(8,128)(2,1)S(1)}, u32[]{:S(2)}, u32[]{:S(2)}) collective-permute-start(bf16[256,384]{0,1:T(8,128)(2,1)} %convert_element_type.149), channel_id=1, source_target_pairs={{0,2},{1,3},{2,4},{3,5},{4,6},{5,7},{6,8},{7,9},{8,10},{9,11},{10,... | collective-permute-start | bytes 589832 | tf_op jit(solution)/shard_map/ppermute | solution.py:16
  68.2 29.4 %collective-permute-start.4 = (bf16[256,384]{0,1:T(8,128)(2,1)}, bf16[256,384]{0,1:T(8,128)(2,1)}, u32[]{:S(2)}, u32[]{:S(2)}) collective-permute-start(bf16[256,384]{0,1:T(8,128)(2,1)} %convert_element_type.149), channel_id=1, source_target_pairs={{2,0},{3,1},{4,2},{5,3},{6,4},{7,5},{8,6},{9,7},{10,8},{11,9},{12,... | collective-permute-start | bytes 589832 | tf_op jit(solution)/shard_map/ppermute | solution.py:16
  70.4 19.4 %collective-permute-start.2 = (bf16[256,384]{0,1:T(8,128)(2,1)}, bf16[256,384]{0,1:T(8,128)(2,1)}, u32[]{:S(2)}, u32[]{:S(2)}) collective-permute-start(bf16[256,384]{0,1:T(8,128)(2,1)} %convert_element_type.149), channel_id=1, source_target_pairs={{0,1},{1,2},{2,3},{3,4},{4,5},{5,6},{6,7},{7,8},{8,9},{9,10},{10,1... | collective-permute-start | bytes 589832 | tf_op jit(solution)/shard_map/ppermute | solution.py:16
  76.4 33.9 %copy-start.19 = (pred[256,256]{0,1:T(8,128)(4,1)S(1)}, pred[256,256]{0,1:T(8,128)(4,1)}, u32[]{:S(2)}) copy-start(pred[256,256]{0,1:T(8,128)(4,1)} %bitcast_compare_fusion.1) | copy-start | bytes 196612
  76.4 34.3 %copy-start.30 = (f32[1,2,2,128]{3,1,2,0:T(2,128)S(1)}, f32[1,2,2,128]{3,1,2,0:T(2,128)}, u32[]{:S(2)}) copy-start(f32[1,2,2,128]{3,1,2,0:T(2,128)} %copy-done.29) | copy-start | bytes 6148
  76.4 34.3 %copy-start.28 = (f32[1,2,2,128]{3,1,2,0:T(2,128)S(1)}, f32[1,2,2,128]{3,1,2,0:T(2,128)}, u32[]{:S(2)}) copy-start(f32[1,2,2,128]{3,1,2,0:T(2,128)} %copy-done.27) | copy-start | bytes 6148
  76.4 35.4 %copy-start.18 = (pred[256,256]{0,1:T(8,128)(4,1)S(1)}, pred[256,256]{0,1:T(8,128)(4,1)}, u32[]{:S(2)}) copy-start(pred[256,256]{0,1:T(8,128)(4,1)} %bitcast_compare_fusion) | copy-start | bytes 196612
  76.4 35.8 %copy-start.32 = (f32[1,2,2,128]{3,1,2,0:T(2,128)S(1)}, f32[1,2,2,128]{3,1,2,0:T(2,128)}, u32[]{:S(2)}) copy-start(f32[1,2,2,128]{3,1,2,0:T(2,128)} %copy-done.31) | copy-start | bytes 6148
  76.4 35.8 %copy-start.35 = (f32[1,2,2,128]{3,1,2,0:T(2,128)S(1)}, f32[1,2,2,128]{3,1,2,0:T(2,128)}, u32[]{:S(2)}) copy-start(f32[1,2,2,128]{3,1,2,0:T(2,128)} %copy-done.34) | copy-start | bytes 6148
  76.5 17.8 %collective-permute-start = (bf16[256,384]{0,1:T(8,128)(2,1)}, bf16[256,384]{0,1:T(8,128)(2,1)S(1)}, u32[]{:S(2)}, u32[]{:S(2)}) collective-permute-start(bf16[256,384]{0,1:T(8,128)(2,1)} %convert_element_type.149), channel_id=1, source_target_pairs={{1,0},{2,1},{3,2},{4,3},{5,4},{6,5},{7,6},{8,7},{9,8},{10,9},{11,1... | collective-permute-start | bytes 589832 | tf_op jit(solution)/shard_map/ppermute | solution.py:16
  78.3 32.1 %collective-permute-start.12 = (bf16[256,384]{0,1:T(8,128)(2,1)}, bf16[256,384]{0,1:T(8,128)(2,1)S(1)}, u32[]{:S(2)}, u32[]{:S(2)}) collective-permute-start(bf16[256,384]{0,1:T(8,128)(2,1)} %convert_element_type.149), channel_id=1, source_target_pairs={{4,0},{5,1},{6,2},{7,3},{8,4},{9,5},{10,6},{11,7},{12,8},{13,9},{1... | collective-permute-start | bytes 589832 | tf_op jit(solution)/shard_map/ppermute | solution.py:16
  80.8 31.0 %collective-permute-start.14 = (bf16[256,384]{0,1:T(8,128)(2,1)}, bf16[256,384]{0,1:T(8,128)(2,1)S(1)}, u32[]{:S(2)}, u32[]{:S(2)}) collective-permute-start(bf16[256,384]{0,1:T(8,128)(2,1)} %convert_element_type.149), channel_id=1, source_target_pairs={{0,4},{1,5},{2,6},{3,7},{4,8},{5,9},{6,10},{7,11},{8,12},{9,13},{1... | collective-permute-start | bytes 589832 | tf_op jit(solution)/shard_map/ppermute | solution.py:16
  89.7 10.7 %copy-start = (f32[256,3,256]{0,2,1:T(8,128)}, f32[256,3,256]{0,2,1:T(8,128)S(1)}, u32[]{:S(2)}) copy-start(f32[256,3,256]{0,2,1:T(8,128)S(1)} %get-tuple-element.58) | copy-start | bytes 2359300
  89.7 22.5 %copy-start.21 = (f32[256,3]{0,1:T(4,128)}, f32[256,3]{0,1:T(4,128)S(1)}, u32[]{:S(2)}) copy-start(f32[256,3]{0,1:T(4,128)S(1)} %get-tuple-element.57) | copy-start | bytes 9220
  91.2 6.5 %copy-start.22 = (f32[256,3]{0,1:T(4,128)}, f32[256,3]{0,1:T(4,128)S(1)}, u32[]{:S(2)}) copy-start(f32[256,3]{0,1:T(4,128)S(1)} %get-tuple-element.61) | copy-start | bytes 9220
  91.2 10.1 %copy-start.1 = (f32[256,3,256]{0,2,1:T(8,128)}, f32[256,3,256]{0,2,1:T(8,128)S(1)}, u32[]{:S(2)}) copy-start(f32[256,3,256]{0,2,1:T(8,128)S(1)} %get-tuple-element.62) | copy-start | bytes 2359300
  96.1 1.6 copy-start.6
  99.0 11.4 %copy-start.3 = (f32[256,3,256]{0,2,1:T(8,128)}, f32[256,3,256]{0,2,1:T(8,128)S(1)}, u32[]{:S(2)}) copy-start(f32[256,3,256]{0,2,1:T(8,128)S(1)} %get-tuple-element.60) | copy-start | bytes 2359300
  99.0 13.3 %copy-start.23 = (f32[256,3]{0,1:T(4,128)}, f32[256,3]{0,1:T(4,128)S(1)}, u32[]{:S(2)}) copy-start(f32[256,3]{0,1:T(4,128)S(1)} %get-tuple-element.59) | copy-start | bytes 9220
  99.7 12.1 %copy-start.10 = (f32[256,2,128]{0,2,1:T(8,128)}, f32[256,2,128]{0,2,1:T(8,128)S(1)}, u32[]{:S(2)}) copy-start(f32[256,2,128]{0,2,1:T(8,128)S(1)} %broadcast_in_dim.165) | copy-start | bytes 786436
  100.4 11.4 %copy-start.9 = (f32[256,2,128]{0,2,1:T(8,128)}, f32[256,2,128]{0,2,1:T(8,128)S(1)}, u32[]{:S(2)}) copy-start(f32[256,2,128]{0,2,1:T(8,128)S(1)} %broadcast_in_dim.168) | copy-start | bytes 786436
  110.7 1.6 copy-start.2
  110.7 1.6 copy-start.24
  208.5 15.6 %copy-start.16 = (bf16[256,384]{0,1:T(8,128)(2,1)S(1)}, bf16[256,384]{0,1:T(8,128)(2,1)}, u32[]{:S(2)}) copy-start(bf16[256,384]{0,1:T(8,128)(2,1)} %copy.106) | copy-start | bytes 589828
  210.3 13.3 %copy-start.5 = (f32[256,3,256]{0,2,1:T(8,128)S(1)}, f32[256,3,256]{0,2,1:T(8,128)}, u32[]{:S(2)}) copy-start(f32[256,3,256]{0,2,1:T(8,128)} %copy-done.4) | copy-start | bytes 2359300
  210.3 13.3 %copy-start.14 = (f32[256,2,128]{0,2,1:T(8,128)S(1)}, f32[256,2,128]{0,2,1:T(8,128)}, u32[]{:S(2)}) copy-start(f32[256,2,128]{0,2,1:T(8,128)} %copy-done.13) | copy-start | bytes 786436
  210.3 13.3 %copy-start.17 = (bf16[256,384]{0,1:T(8,128)(2,1)S(1)}, bf16[256,384]{0,1:T(8,128)(2,1)}, u32[]{:S(2)}) copy-start(bf16[256,384]{0,1:T(8,128)(2,1)} %copy.141) | copy-start | bytes 589828
  210.3 13.3 %copy-start.26 = (f32[256,3]{0,1:T(4,128)S(1)}, f32[256,3]{0,1:T(4,128)}, u32[]{:S(2)}) copy-start(f32[256,3]{0,1:T(4,128)} %copy-done.25) | copy-start | bytes 9220
  210.3 13.8 %copy-start.7 = (f32[256,2,128]{0,2,1:T(8,128)S(1)}, f32[256,2,128]{0,2,1:T(8,128)}, u32[]{:S(2)}) copy-start(f32[256,2,128]{0,2,1:T(8,128)} %copy-done.6) | copy-start | bytes 786436
  (8 other events, 8.0 us)
Sparse Core Ops, SparseCore 0:
  14.8 181.1 all-gather.2
